TPU v7x, 32 devices: a whole 2x2x4 slice. The times are simulated.
32 devices in a mesh: span: 8 (over z, x), chord: 4 (over y, core).
Axes of the slice: x: 2, y: 2, z: 4, core: 2. Of those that a mesh axis runs over, the one named last changes fastest.
Arguments:
- pressure: float32 [2, 1024, 512], P(None, 'span', 'chord'), may hold values from 0 to 1
- fill_state: int32 [2, 1024, 512], P(None, 'span', 'chord'), may hold values from 0 to 2
- perm_class: int32 [2, 1024, 512], P(None, 'span', 'chord'), may hold values from 0 to 7
- perm_table: float32 [2, 8], replicated, may hold values from 1 to 4
- inlet_span: int32 [128], replicated, may hold values from 0 to 1023
- inlet_chord: int32 [128], replicated, may hold values from 0 to 511
- inlet_rate: float32 [128], replicated, may hold values from 500 to 1500
Outputs:
- pressure_out: float32 [2, 1024, 512], P(None, 'span', 'chord')
Inputs may be any that keep to these rules, and one draw needn't show every extreme that they name: `inlet_span`: inlet cells may repeat; their rates add.
All inputs are finite; a program needn't handle non-finite values.
Results may differ from a plain program's by a relative error of at most 0.00035.
Values sent between devices are 32-bit elements; how exact they have to be, the bound alone decides.
A program may use at most 64 MiB of HBM per device.

v0:
```python
import functools

import jax
import jax.numpy as jnp
from jax import lax
from jax.experimental import pallas as pl
from jax.experimental.pallas import tpu as pltpu
from jax.sharding import PartitionSpec as P

HALF_RATE = 200.0
COUPLE = 0.3
MESH = pl.DeviceIdType.MESH
TILE = 8
LIMIT = 16 << 20


def down(x, s):
    if s % TILE == 0:
        return jnp.concatenate([x[-s:], x[:-s]], axis=0)
    return pltpu.roll(x, s, 0)


def up(x, s):
    if s % TILE == 0:
        return jnp.concatenate([x[s:], x[:s]], axis=0)
    return pltpu.roll(x, x.shape[0] - s, 0)


def from_row(s, value, other):
    if s % TILE == 0:
        return jnp.concatenate([other[:s], value[s:]], axis=0)
    rows = lax.broadcasted_iota(jnp.int32, value.shape, 0)
    return jnp.where(rows >= s, value, other)


def to_row(s, value, other):
    n = value.shape[0]
    if s % TILE == 0:
        return jnp.concatenate([value[: n - s], other[n - s :]], axis=0)
    rows = lax.broadcasted_iota(jnp.int32, value.shape, 0)
    return jnp.where(rows < n - s, value, other)


def factor(cond, keep):
    n = cond.shape[0]
    zero = jnp.zeros_like(cond)
    one = jnp.ones_like(cond)
    g = HALF_RATE * (cond + up(cond, 1))
    a = from_row(1, down(g, 1), one)
    c = to_row(1, g, one)
    e = one
    s, k = 1, 0
    while s < n:
        a_in = from_row(s, a, zero)
        c_in = to_row(s, c, zero)
        rb = 1.0 / (e + a_in + c_in)
        al = a_in * down(rb, s)
        be = c_in * up(rb, s)
        keep(k, al, be)
        a = from_row(s, al * down(a, s), a)
        c = to_row(s, be * up(c, s), c)
        e = e + al * down(e, s) + be * up(e, s)
        s, k = 2 * s, k + 1
    re = 1.0 / e
    return a * re, c * re, re


def reduce_rhs(d, kept, re):
    n = d.shape[0]
    s, k = 1, 0
    while s < n:
        al, be = kept(k)
        if s % TILE == 0:
            zero = jnp.zeros_like(d[:s])
            d = (
                d
                + jnp.concatenate([zero, al[s:] * d[:-s]], axis=0)
                + jnp.concatenate([be[:-s] * d[s:], zero], axis=0)
            )
        else:
            d = d + al * down(d, s) + be * up(d, s)
        s, k = 2 * s, k + 1
    return d * re


class Gather:
    def __init__(self, axis, n, me, buf, send, recv):
        self.copies = []
        self.landed = []
        for o in range(1, n):
            dst = lax.rem(me + o, n)
            src = lax.rem(me + n - o, n)
            self.copies.append(
                pltpu.make_async_remote_copy(
                    buf.at[me], buf.at[me], send.at[o], recv.at[o], {axis: dst}, MESH
                )
            )
            self.landed.append(
                pltpu.make_async_remote_copy(
                    buf.at[src], buf.at[src], send.at[o], recv.at[o], {axis: dst}, MESH
                )
            )

    def start(self):
        for copy in self.copies:
            copy.start()

    def wait(self):
        for copy in self.landed:
            copy.wait_recv()

    def wait_sent(self):
        for copy in self.copies:
            copy.wait_send()


def put_coefs(buf, me, plies, p, A, C, cond):
    n = A.shape[0]
    values = (A[:1], C[n - 1 :], A[n - 1 :], cond[:1], cond[n - 1 :])
    for q, v in enumerate(values):
        buf[me, q * plies + p : q * plies + p + 1, :] = v


def flux_factor(buf, n, plies):
    def at(j, q):
        return buf[j, q * plies : (q + 1) * plies, :]

    w, m = [None] * (n + 1), [None] * (n + 1)
    cross = [at(j, 2) for j in range(n)]
    for j in range(1, n):
        diag = 1.0 / (HALF_RATE * (at(j - 1, 4) + at(j, 3))) + at(j - 1, 1) + at(j, 0)
        if j > 1:
            m[j] = cross[j - 1] * w[j - 1]
            diag = diag - cross[j - 1] * m[j]
        w[j] = 1.0 / diag
    return w, m, cross


def flux_solve(buf, n, plies, me, w, m, cross):
    y = [None] * (n + 1)
    for j in range(1, n):
        r = buf[j - 1, plies : 2 * plies, :] - buf[j, :plies, :]
        y[j] = r if j == 1 else r + m[j] * y[j - 1]
    zero = jnp.zeros((plies, buf.shape[-1]), jnp.float32)
    top, bottom = zero, zero
    flux = None
    for j in range(n - 1, 0, -1):
        flux = w[j] * (y[j] if flux is None else y[j] + cross[j] * flux)
        top = jnp.where(me == j, flux, top)
        bottom = jnp.where(me + 1 == j, flux, bottom)
    return top, bottom


def kernel(
    ns, nc, plies, classes,
    pressure_hbm, fill_hbm, class_hbm, table_hbm, span_hbm, chord_hbm, rate_hbm,
    D_c, A_c, C_c, flux_ref,
    pressure, fill, klass, table_ref, span_ref, chord_ref, rate_ref, half, keep_s, keep_c, A_s, C_s, E_s, E_c, D, sides,
    halo_out, halo_in, coef_s, coef_c, edge_s, edge_c,
    load_sem, halo_send, halo_recv,
    cs_send, cs_recv, cc_send, cc_recv, es_send, es_recv, ec_send, ec_recv,
):
    rows, width = pressure.shape[1:]
    me_s, me_c = lax.axis_index("span"), lax.axis_index("chord")
    barrier = pltpu.get_barrier_semaphore()
    for o in range(1, nc):
        pl.semaphore_signal(
            barrier, inc=1, device_id={"chord": lax.rem(me_c + o, nc)}, device_id_type=MESH
        )
    loads = [
        pltpu.make_async_copy(src, dst, load_sem.at[i])
        for i, (src, dst) in enumerate(
            (
                (class_hbm, klass), (fill_hbm, fill), (pressure_hbm, pressure), (table_hbm, table_ref),
                (span_hbm, span_ref), (chord_hbm, chord_ref), (rate_hbm, rate_ref),
            )
        )
    ]
    for load in loads:
        load.start()
    for o in range(1, ns):
        pl.semaphore_signal(
            barrier, inc=1, device_id={"span": lax.rem(me_s + o, ns)}, device_id_type=MESH
        )

    for load in loads:
        load.wait()

    conds, turned, fields = [], [], []
    for p in range(plies):
        perm = jnp.full((rows, width), table_ref[p, 0], jnp.float32)
        kl = klass[p]
        for k in range(1, classes):
            perm = jnp.where(kl == k, table_ref[p, k], perm)
        st = fill[p]
        cond = perm * jnp.where(st == 0, 1.0, jnp.where(st == 1, 0.5, 0.25))
        conds.append(cond)
        turned.append(cond.T)
        fields.append(pressure[p].T)
        for side, at in ((0, 0), (1, width - 1)):
            halo_out[side, p : p + 1, :] = turned[p][at : at + 1]
            halo_out[side, plies + p : plies + p + 1, :] = fields[p][at : at + 1]

    pl.semaphore_wait(barrier, ns + nc - 2)
    ahead, behind = lax.rem(me_c + 1, nc), lax.rem(me_c + nc - 1, nc)
    halos = [
        pltpu.make_async_remote_copy(
            halo_out.at[side], halo_in.at[side], halo_send.at[side], halo_recv.at[side],
            {"chord": to}, MESH,
        )
        for side, to in ((0, behind), (1, ahead))
    ]
    for copy in halos:
        copy.start()

    def keeper(ref, p):
        def keep(k, al, be):
            ref[k, 0, p] = al
            ref[k, 1, p] = be

        return keep

    def kept(ref, p):
        return lambda k: (ref[k, 0, p], ref[k, 1, p])

    for p in range(plies):
        A, C, re = factor(conds[p], keeper(keep_s, p))
        A_s[p], C_s[p], E_s[p] = A, C, re
        put_coefs(coef_s, me_s, plies, p, A, C, conds[p])
    span_coefs = Gather("span", ns, me_s, coef_s, cs_send, cs_recv)
    span_coefs.start()

    row_id = lax.broadcasted_iota(jnp.int32, (rows, span_ref.shape[1]), 0) + me_s * rows
    col_id = lax.broadcasted_iota(jnp.int32, (width, span_ref.shape[1]), 0) + me_c * width
    row_hits = jnp.where(row_id == span_ref[...], rate_ref[...], 0.0)
    col_hits = jnp.where(col_id == chord_ref[...], 1.0, 0.0)
    plane = lax.dot_general(
        row_hits, col_hits, (((1,), (1,)), ((), ())),
        precision=lax.Precision.HIGHEST, preferred_element_type=jnp.float32,
    )

    explicit = []
    for p in range(plies):
        f, other = fields[p], fields[plies - 1 - p]
        g = HALF_RATE * (turned[p] + up(turned[p], 1))
        flow = to_row(1, g * (up(f, 1) - f), jnp.zeros_like(f))
        back = from_row(1, down(flow, 1), jnp.zeros_like(f))
        explicit.append(f + (flow - back) + COUPLE * (other - f))

    for p in range(plies):
        rhs = explicit[p].T + plane
        half[p] = rhs
        d = reduce_rhs(rhs, kept(keep_s, p), E_s[p])
        edge_s[me_s, p : p + 1, :] = d[:1]
        edge_s[me_s, plies + p : plies + p + 1, :] = d[rows - 1 :]
        for q, response in enumerate((A_s[p].T, C_s[p].T)):
            sides[2 * q, p : p + 1, :] = response[:1]
            sides[2 * q + 1, p : p + 1, :] = response[width - 1 :]

    for copy in halos:
        copy.wait_recv()

    def inflow(mine, theirs):
        conds_sum = halo_in[theirs, :plies, :] + halo_out[mine, :plies, :]
        return HALF_RATE * conds_sum * (halo_in[theirs, plies:, :] - halo_out[mine, plies:, :])

    first = jnp.where(me_c > 0, inflow(0, 1), 0.0)
    last = jnp.where(me_c < nc - 1, inflow(1, 0), 0.0)
    lane = lax.broadcasted_iota(jnp.int32, (plies, width), 1)
    for q in range(2):
        by_first = jnp.sum(sides[2 * q] * first, axis=1, keepdims=True)
        by_last = jnp.sum(sides[2 * q + 1] * last, axis=1, keepdims=True)
        edge_s[me_s, q * plies : (q + 1) * plies, :] = (
            edge_s[me_s, q * plies : (q + 1) * plies, :]
            + jnp.where(lane == 0, by_first, 0.0)
            + jnp.where(lane == width - 1, by_last, 0.0)
        )
    span_edges = Gather("span", ns, me_s, edge_s, es_send, es_recv)
    span_edges.start()

    lanes = lax.broadcasted_iota(jnp.int32, (width, rows), 0)
    for p in range(plies):
        change = jnp.where(lanes == 0, first[p : p + 1], 0.0) + jnp.where(
            lanes == width - 1, last[p : p + 1], 0.0
        )
        rhs = half[p] + change.T
        half[p] = rhs
        D[p] = reduce_rhs(rhs, kept(keep_s, p), E_s[p])

    for p in range(plies):
        A, C, re = factor(turned[p], keeper(keep_c, p))
        A_c[p], C_c[p], E_c[p] = A, C, re
        put_coefs(coef_c, me_c, plies, p, A, C, turned[p])
    chord_coefs = Gather("chord", nc, me_c, coef_c, cc_send, cc_recv)
    chord_coefs.start()

    span_coefs.wait()
    parts = flux_factor(coef_s, ns, plies)
    span_edges.wait()
    top, bottom = flux_solve(edge_s, ns, plies, me_s, *parts)
    stars = [D[p] + A_s[p] * top[p : p + 1] - C_s[p] * bottom[p : p + 1] for p in range(plies)]
    for p in range(plies):
        star, other = stars[p], stars[plies - 1 - p]
        second = 2.0 * star - half[p] + COUPLE * (other - star) + plane
        d = reduce_rhs(second.T, kept(keep_c, p), E_c[p])
        D_c[p] = d
        edge_c[me_c, p : p + 1, :] = d[:1]
        edge_c[me_c, plies + p : plies + p + 1, :] = d[width - 1 :]
    chord_edges = Gather("chord", nc, me_c, edge_c, ec_send, ec_recv)
    chord_edges.start()

    chord_coefs.wait()
    parts = flux_factor(coef_c, nc, plies)
    for copy in halos:
        copy.wait_send()
    for gather in (span_coefs, chord_coefs, span_edges):
        gather.wait_sent()
    chord_edges.wait()
    flux_ref[0], flux_ref[1] = flux_solve(edge_c, nc, plies, me_c, *parts)
    chord_edges.wait_sent()


def finish(plies, D_c, A_c, C_c, flux_ref, out_hbm, block, sem):
    copies = []
    for p in range(plies):
        top, bottom = flux_ref[0, p : p + 1, :], flux_ref[1, p : p + 1, :]
        block[p] = (D_c[p] + A_c[p] * top - C_c[p] * bottom).T
        copies.append(pltpu.make_async_copy(block.at[p], out_hbm.at[p], sem.at[p]))
        copies[-1].start()
    for copy in copies:
        copy.wait()


def levels(n):
    return max(1, (n - 1).bit_length())


def per_device(ns, nc, pressure, fill_state, perm_class, perm_table, inlet_span, inlet_chord, inlet_rate):
    plies, rows, width = pressure.shape
    classes = perm_table.shape[1]
    inlets = inlet_span.shape[0]
    vmem = pl.BlockSpec(memory_space=pltpu.VMEM)
    hbm = pl.BlockSpec(memory_space=pltpu.HBM)
    f32 = jnp.float32
    block = pltpu.VMEM((plies, rows, width), f32)
    block_t = pltpu.VMEM((plies, width, rows), f32)
    iblock = pltpu.VMEM((plies, rows, width), jnp.int32)
    dma = lambda n: pltpu.SemaphoreType.DMA((n,))
    lines = pltpu.VMEM((plies, width, rows), f32)
    solved = pl.pallas_call(
        functools.partial(kernel, ns, nc, plies, classes),
        out_shape=(lines, lines, lines, pltpu.VMEM((2, plies, rows), f32)),
        in_specs=[hbm] * 7,
        out_specs=(vmem,) * 4,
        scratch_shapes=[
            block, iblock, iblock,
            pltpu.SMEM(perm_table.shape, f32),
            pltpu.VMEM((1, inlets), jnp.int32), pltpu.VMEM((1, inlets), jnp.int32), pltpu.VMEM((1, inlets), f32),
            block,
            pltpu.VMEM((levels(rows), 2, plies, rows, width), f32),
            pltpu.VMEM((levels(width), 2, plies, width, rows), f32),
            block, block, block, block_t, block,
            pltpu.VMEM((4, plies, rows), f32),
            pltpu.VMEM((2, 2 * plies, rows), f32),
            pltpu.VMEM((2, 2 * plies, rows), f32),
            pltpu.VMEM((ns, 5 * plies, width), f32),
            pltpu.VMEM((nc, 5 * plies, rows), f32),
            pltpu.VMEM((ns, 2 * plies, width), f32),
            pltpu.VMEM((nc, 2 * plies, rows), f32),
            dma(7), dma(2), dma(2),
            dma(ns), dma(ns), dma(nc), dma(nc), dma(ns), dma(ns), dma(nc), dma(nc),
        ],
        compiler_params=pltpu.CompilerParams(collective_id=0, has_side_effects=True, vmem_limit_bytes=LIMIT),
    )(
        *(
            pltpu.with_memory_space_constraint(x, pltpu.HBM)
            for x in (
                pressure, fill_state, perm_class, perm_table, inlet_span.reshape(1, inlets),
                inlet_chord.reshape(1, inlets), inlet_rate.reshape(1, inlets),
            )
        )
    )
    return pl.pallas_call(
        functools.partial(finish, plies),
        out_shape=jax.ShapeDtypeStruct(pressure.shape, f32),
        in_specs=[vmem] * 4,
        out_specs=hbm,
        scratch_shapes=[block, dma(plies)],
        compiler_params=pltpu.CompilerParams(vmem_limit_bytes=LIMIT),
    )(*solved)


def solution(mesh):
    block = P(None, "span", "chord")
    return jax.shard_map(
        functools.partial(per_device, mesh.shape["span"], mesh.shape["chord"]),
        mesh=mesh,
        in_specs=(block, block, block, P(), P(), P(), P()),
        out_specs=block,
        check_vma=False,
    )
```

profile of v0, /device:TPU:0, one launch (start us, length us, event | category | flops | bytes accessed | tf_op | source)
XLA Modules:
  0.0 15.4 jit_solution(15144465632626264933)
XLA Ops:
  0.0 14.6 %shard_map.73 = (f32[2,128,128]{2,1,0:T(8,128)S(1)}, f32[2,128,128]{2,1,0:T(8,128)S(1)}, f32[2,128,128]{2,1,0:T(8,128)S(1)}, f32[2,2,128]{2,1,0:T(2,128)S(1)}) custom-call(f32[2,128,128]{2,1,0:T(8,128)} %pressure_hbm.1, s32[2,128,128]{2,1,0:T(8,128)} %fill_hbm.1, s32[2,128,128]{2,1,0:T(8,128)} %class_hbm.1, f32[2,8]{1,0:T(2,128)} %table_hbm.1, ...), custom_call_target="tpu_custom_call" | custom-call | tf_op jit(solution)/shard_map/pallas_call | solution.py:350
  14.6 0.8 %shard_map.74 = f32[2,128,128]{2,1,0:T(8,128)} custom-call(f32[2,128,128]{2,1,0:T(8,128)S(1)} %get-tuple-element.9.D_c, f32[2,128,128]{2,1,0:T(8,128)S(1)} %get-tuple-element.10.A_c, f32[2,128,128]{2,1,0:T(8,128)S(1)} %get-tuple-element.11.C_c, f32[2,2,128]{2,1,0:T(2,128)S(1)} %get-tuple-element.12.flux_ref), custom_call_target="tpu_custom_call" | custom-call | tf_op jit(solution)/shard_map/pallas_call | solution.py:383
where the time goes:
time: 15.5 us; the launch traced here: 15.4 us
  Pallas kernels  15.4 us (99%)
    pallas_call x1, Pallas kernels, per_device(): pl.pallas_call(functools.partial(kernel, ns, nc, plies, classes), out_sha...  14.6 us
    pallas_call x1, Pallas kernels, per_device(): pl.pallas_call(functools.partial(finish, plies), out_shape=jax.ShapeDtype...  0.78 us

commit v1 on v0

--- a/solution.py
+++ b/solution.py
@@ -86,32 +86,23 @@
 class Gather:
     def __init__(self, axis, n, me, buf, send, recv):
         self.copies = []
-        self.landed = []
         for o in range(1, n):
             dst = lax.rem(me + o, n)
-            src = lax.rem(me + n - o, n)
             self.copies.append(
-                pltpu.make_async_remote_copy(
-                    buf.at[me], buf.at[me], send.at[o], recv.at[o], {axis: dst}, MESH
-                )
+                pltpu.make_async_remote_copy(buf.at[me], buf.at[me], send, recv, {axis: dst}, MESH)
             )
-            self.landed.append(
-                pltpu.make_async_remote_copy(
-                    buf.at[src], buf.at[src], send.at[o], recv.at[o], {axis: dst}, MESH
-                )
-            )
+        many = buf.at[pl.ds(0, n - 1)]
+        self.all = pltpu.make_async_remote_copy(many, many, send, recv, {axis: lax.rem(me + 1, n)}, MESH)
 
     def start(self):
         for copy in self.copies:
             copy.start()
 
     def wait(self):
-        for copy in self.landed:
-            copy.wait_recv()
+        self.all.wait_recv()
 
     def wait_sent(self):
-        for copy in self.copies:
-            copy.wait_send()
+        self.all.wait_send()
 
 
 def put_coefs(buf, me, plies, p, A, C, cond):
@@ -155,10 +146,9 @@
     ns, nc, plies, classes,
     pressure_hbm, fill_hbm, class_hbm, table_hbm, span_hbm, chord_hbm, rate_hbm,
     D_c, A_c, C_c, flux_ref,
-    pressure, fill, klass, table_ref, span_ref, chord_ref, rate_ref, half, keep_s, keep_c, A_s, C_s, E_s, E_c, D, sides,
+    pressure, state, table_ref, inlet_ref, rate_ref, half, keep_s, keep_c, A_s, C_s, E_s, E_c, D, sides,
     halo_out, halo_in, coef_s, coef_c, edge_s, edge_c,
-    load_sem, halo_send, halo_recv,
-    cs_send, cs_recv, cc_send, cc_recv, es_send, es_recv, ec_send, ec_recv,
+    sent, landed,
 ):
     rows, width = pressure.shape[1:]
     me_s, me_c = lax.axis_index("span"), lax.axis_index("chord")
@@ -168,12 +158,11 @@
             barrier, inc=1, device_id={"chord": lax.rem(me_c + o, nc)}, device_id_type=MESH
         )
     loads = [
-        pltpu.make_async_copy(src, dst, load_sem.at[i])
-        for i, (src, dst) in enumerate(
-            (
-                (class_hbm, klass), (fill_hbm, fill), (pressure_hbm, pressure), (table_hbm, table_ref),
-                (span_hbm, span_ref), (chord_hbm, chord_ref), (rate_hbm, rate_ref),
-            )
+        pltpu.make_async_copy(src, dst, sent.at[i])
+        for src, dst, i in (
+            (class_hbm, state.at[0], 0), (fill_hbm, state.at[1], 0), (pressure_hbm, pressure, 1),
+            (table_hbm, table_ref, 2), (span_hbm, inlet_ref.at[0], 3), (chord_hbm, inlet_ref.at[1], 3),
+            (rate_hbm, rate_ref, 4),
         )
     ]
     for load in loads:
@@ -183,16 +172,19 @@
             barrier, inc=1, device_id={"span": lax.rem(me_s + o, ns)}, device_id_type=MESH
         )
 
-    for load in loads:
-        load.wait()
+    pltpu.make_async_copy(state, state, sent.at[0]).wait()
+    pltpu.make_async_copy(pressure, pressure, sent.at[1]).wait()
+    loads[3].wait()
+    pltpu.make_async_copy(inlet_ref, inlet_ref, sent.at[3]).wait()
+    loads[6].wait()
 
     conds, turned, fields = [], [], []
     for p in range(plies):
         perm = jnp.full((rows, width), table_ref[p, 0], jnp.float32)
-        kl = klass[p]
+        kl = state[0, p]
         for k in range(1, classes):
             perm = jnp.where(kl == k, table_ref[p, k], perm)
-        st = fill[p]
+        st = state[1, p]
         cond = perm * jnp.where(st == 0, 1.0, jnp.where(st == 1, 0.5, 0.25))
         conds.append(cond)
         turned.append(cond.T)
@@ -205,13 +197,16 @@
     ahead, behind = lax.rem(me_c + 1, nc), lax.rem(me_c + nc - 1, nc)
     halos = [
         pltpu.make_async_remote_copy(
-            halo_out.at[side], halo_in.at[side], halo_send.at[side], halo_recv.at[side],
+            halo_out.at[side], halo_in.at[side], sent.at[0], landed.at[0],
             {"chord": to}, MESH,
         )
         for side, to in ((0, behind), (1, ahead))
     ]
     for copy in halos:
         copy.start()
+    both = pltpu.make_async_remote_copy(
+        halo_out, halo_in, sent.at[0], landed.at[0], {"chord": ahead}, MESH
+    )
 
     def keeper(ref, p):
         def keep(k, al, be):
@@ -227,13 +222,13 @@
         A, C, re = factor(conds[p], keeper(keep_s, p))
         A_s[p], C_s[p], E_s[p] = A, C, re
         put_coefs(coef_s, me_s, plies, p, A, C, conds[p])
-    span_coefs = Gather("span", ns, me_s, coef_s, cs_send, cs_recv)
+    span_coefs = Gather("span", ns, me_s, coef_s, sent.at[1], landed.at[1])
     span_coefs.start()
 
-    row_id = lax.broadcasted_iota(jnp.int32, (rows, span_ref.shape[1]), 0) + me_s * rows
-    col_id = lax.broadcasted_iota(jnp.int32, (width, span_ref.shape[1]), 0) + me_c * width
-    row_hits = jnp.where(row_id == span_ref[...], rate_ref[...], 0.0)
-    col_hits = jnp.where(col_id == chord_ref[...], 1.0, 0.0)
+    row_id = lax.broadcasted_iota(jnp.int32, (rows, rate_ref.shape[1]), 0) + me_s * rows
+    col_id = lax.broadcasted_iota(jnp.int32, (width, rate_ref.shape[1]), 0) + me_c * width
+    row_hits = jnp.where(row_id == inlet_ref[0], rate_ref[...], 0.0)
+    col_hits = jnp.where(col_id == inlet_ref[1], 1.0, 0.0)
     plane = lax.dot_general(
         row_hits, col_hits, (((1,), (1,)), ((), ())),
         precision=lax.Precision.HIGHEST, preferred_element_type=jnp.float32,
@@ -257,8 +252,7 @@
             sides[2 * q, p : p + 1, :] = response[:1]
             sides[2 * q + 1, p : p + 1, :] = response[width - 1 :]
 
-    for copy in halos:
-        copy.wait_recv()
+    both.wait_recv()
 
     def inflow(mine, theirs):
         conds_sum = halo_in[theirs, :plies, :] + halo_out[mine, :plies, :]
@@ -275,7 +269,7 @@
             + jnp.where(lane == 0, by_first, 0.0)
             + jnp.where(lane == width - 1, by_last, 0.0)
         )
-    span_edges = Gather("span", ns, me_s, edge_s, es_send, es_recv)
+    span_edges = Gather("span", ns, me_s, edge_s, sent.at[3], landed.at[3])
     span_edges.start()
 
     lanes = lax.broadcasted_iota(jnp.int32, (width, rows), 0)
@@ -291,7 +285,7 @@
         A, C, re = factor(turned[p], keeper(keep_c, p))
         A_c[p], C_c[p], E_c[p] = A, C, re
         put_coefs(coef_c, me_c, plies, p, A, C, turned[p])
-    chord_coefs = Gather("chord", nc, me_c, coef_c, cc_send, cc_recv)
+    chord_coefs = Gather("chord", nc, me_c, coef_c, sent.at[2], landed.at[2])
     chord_coefs.start()
 
     span_coefs.wait()
@@ -306,13 +300,12 @@
         D_c[p] = d
         edge_c[me_c, p : p + 1, :] = d[:1]
         edge_c[me_c, plies + p : plies + p + 1, :] = d[width - 1 :]
-    chord_edges = Gather("chord", nc, me_c, edge_c, ec_send, ec_recv)
+    chord_edges = Gather("chord", nc, me_c, edge_c, sent.at[4], landed.at[4])
     chord_edges.start()
 
     chord_coefs.wait()
     parts = flux_factor(coef_c, nc, plies)
-    for copy in halos:
-        copy.wait_send()
+    both.wait_send()
     for gather in (span_coefs, chord_coefs, span_edges):
         gather.wait_sent()
     chord_edges.wait()
@@ -353,9 +346,9 @@
         in_specs=[hbm] * 7,
         out_specs=(vmem,) * 4,
         scratch_shapes=[
-            block, iblock, iblock,
+            block, pltpu.VMEM((2, plies, rows, width), jnp.int32),
             pltpu.SMEM(perm_table.shape, f32),
-            pltpu.VMEM((1, inlets), jnp.int32), pltpu.VMEM((1, inlets), jnp.int32), pltpu.VMEM((1, inlets), f32),
+            pltpu.VMEM((2, 1, inlets), jnp.int32), pltpu.VMEM((1, inlets), f32),
             block,
             pltpu.VMEM((levels(rows), 2, plies, rows, width), f32),
             pltpu.VMEM((levels(width), 2, plies, width, rows), f32),
@@ -367,8 +360,7 @@
             pltpu.VMEM((nc, 5 * plies, rows), f32),
             pltpu.VMEM((ns, 2 * plies, width), f32),
             pltpu.VMEM((nc, 2 * plies, rows), f32),
-            dma(7), dma(2), dma(2),
-            dma(ns), dma(ns), dma(nc), dma(nc), dma(ns), dma(ns), dma(nc), dma(nc),
+            dma(5), dma(5),
         ],
         compiler_params=pltpu.CompilerParams(collective_id=0, has_side_effects=True, vmem_limit_bytes=LIMIT),
     )(

time: 15.5 us -> 15.1 us (0.974)
  Pallas kernels: 15.4 us -> 14.9 us
    pallas_call x1, Pallas kernels: 14.6 us -> 14.1 us  [per_device(): pl.pallas_call(functools.partial(kernel, ns, nc, plies, classes), out_sha...]
where the time goes in v1:
time: 15.1 us; the launch traced here: 14.9 us
  Pallas kernels  14.9 us (99%)
    pallas_call x1, Pallas kernels, per_device(): pl.pallas_call(functools.partial(kernel, ns, nc, plies, classes), out_sha...  14.1 us
    pallas_call x1, Pallas kernels, per_device(): pl.pallas_call(functools.partial(finish, plies), out_shape=jax.ShapeDtype...  0.78 us

profile of v1, /device:TPU:0, one launch (start us, length us, event | category | flops | bytes accessed | tf_op | source)
XLA Modules:
  0.0 14.9 jit_solution(7720539738476807681)
XLA Ops:
  0.0 14.1 %shard_map.73 = (f32[2,128,128]{2,1,0:T(8,128)S(1)}, f32[2,128,128]{2,1,0:T(8,128)S(1)}, f32[2,128,128]{2,1,0:T(8,128)S(1)}, f32[2,2,128]{2,1,0:T(2,128)S(1)}) custom-call(f32[2,128,128]{2,1,0:T(8,128)} %pressure_hbm.1, s32[2,128,128]{2,1,0:T(8,128)} %fill_hbm.1, s32[2,128,128]{2,1,0:T(8,128)} %class_hbm.1, f32[2,8]{1,0:T(2,128)} %table_hbm.1, ...), custom_call_target="tpu_custom_call" | custom-call | tf_op jit(solution)/shard_map/pallas_call | solution.py:343
  14.2 0.8 %shard_map.74 = f32[2,128,128]{2,1,0:T(8,128)} custom-call(f32[2,128,128]{2,1,0:T(8,128)S(1)} %get-tuple-element.9.D_c, f32[2,128,128]{2,1,0:T(8,128)S(1)} %get-tuple-element.10.A_c, f32[2,128,128]{2,1,0:T(8,128)S(1)} %get-tuple-element.11.C_c, f32[2,2,128]{2,1,0:T(2,128)S(1)} %get-tuple-element.12.flux_ref), custom_call_target="tpu_custom_call" | custom-call | tf_op jit(solution)/shard_map/pallas_call | solution.py:375

commit v2 on v1

v2 whole, which is shorter than its diff:
```python
import functools

import jax
import jax.numpy as jnp
from jax import lax
from jax.experimental import pallas as pl
from jax.experimental.pallas import tpu as pltpu
from jax.sharding import PartitionSpec as P

HALF_RATE = 200.0
COUPLE = 0.3
MESH = pl.DeviceIdType.MESH
TILE = 8
LIMIT = 16 << 20


def down(x, s):
    if s % TILE == 0:
        return jnp.concatenate([x[-s:], x[:-s]], axis=0)
    return pltpu.roll(x, s, 0)


def up(x, s):
    if s % TILE == 0:
        return jnp.concatenate([x[s:], x[:s]], axis=0)
    return pltpu.roll(x, x.shape[0] - s, 0)


def from_row(s, value, other):
    if s % TILE == 0:
        return jnp.concatenate([other[:s], value[s:]], axis=0)
    rows = lax.broadcasted_iota(jnp.int32, value.shape, 0)
    return jnp.where(rows >= s, value, other)


def to_row(s, value, other):
    n = value.shape[0]
    if s % TILE == 0:
        return jnp.concatenate([value[: n - s], other[n - s :]], axis=0)
    rows = lax.broadcasted_iota(jnp.int32, value.shape, 0)
    return jnp.where(rows < n - s, value, other)


def factor(cond, keep):
    n = cond.shape[0]
    zero = jnp.zeros_like(cond)
    one = jnp.ones_like(cond)
    g = HALF_RATE * (cond + up(cond, 1))
    a = from_row(1, down(g, 1), one)
    c = to_row(1, g, one)
    e = one
    s, k = 1, 0
    while s < n:
        a_in = from_row(s, a, zero)
        c_in = to_row(s, c, zero)
        rb = 1.0 / (e + a_in + c_in)
        al = a_in * down(rb, s)
        be = c_in * up(rb, s)
        keep(k, al, be)
        a = from_row(s, al * down(a, s), a)
        c = to_row(s, be * up(c, s), c)
        e = e + al * down(e, s) + be * up(e, s)
        s, k = 2 * s, k + 1
    re = 1.0 / e
    return a * re, c * re, re


def reduce_rhs(d, kept, re):
    n = d.shape[0]
    s, k = 1, 0
    while s < n:
        al, be = kept(k)
        if s % TILE == 0:
            zero = jnp.zeros_like(d[:s])
            d = (
                d
                + jnp.concatenate([zero, al[s:] * d[:-s]], axis=0)
                + jnp.concatenate([be[:-s] * d[s:], zero], axis=0)
            )
        else:
            d = d + al * down(d, s) + be * up(d, s)
        s, k = 2 * s, k + 1
    return d * re


def others(n, me):
    return [k + (me <= k).astype(jnp.int32) for k in range(n - 1)]


class Gather:
    def __init__(self, axis, n, me, buf, send, recv):
        targets = others(n, me)
        self.copies = [
            pltpu.make_async_remote_copy(buf.at[me], buf.at[me], send, recv, {axis: to}, MESH)
            for to in targets
        ]
        many = buf.at[pl.ds(0, n - 1)]
        self.all = pltpu.make_async_remote_copy(many, many, send, recv, {axis: targets[0]}, MESH)

    def start(self):
        for copy in self.copies:
            copy.start()

    def wait(self):
        self.all.wait_recv()

    def wait_sent(self):
        self.all.wait_send()


def put_coefs(buf, me, plies, p, A, C, cond):
    n = A.shape[0]
    values = (A[:1], C[n - 1 :], A[n - 1 :], cond[:1], cond[n - 1 :])
    for q, v in enumerate(values):
        buf[me, q * plies + p : q * plies + p + 1, :] = v


def flux_factor(buf, n, plies):
    def at(j, q):
        return buf[j, q * plies : (q + 1) * plies, :]

    w, m = [None] * (n + 1), [None] * (n + 1)
    cross = [at(j, 2) for j in range(n)]
    for j in range(1, n):
        diag = 1.0 / (HALF_RATE * (at(j - 1, 4) + at(j, 3))) + at(j - 1, 1) + at(j, 0)
        if j > 1:
            m[j] = cross[j - 1] * w[j - 1]
            diag = diag - cross[j - 1] * m[j]
        w[j] = 1.0 / diag
    return w, m, cross


def flux_solve(buf, n, plies, me, w, m, cross, fix=None):
    y = [None] * (n + 1)
    for j in range(1, n):
        r = buf[j - 1, plies : 2 * plies, :] - buf[j, :plies, :]
        if fix is not None:
            r = r + fix[j]
        y[j] = r if j == 1 else r + m[j] * y[j - 1]
    zero = jnp.zeros((plies, buf.shape[-1]), jnp.float32)
    top, bottom = zero, zero
    flux = None
    for j in range(n - 1, 0, -1):
        flux = w[j] * (y[j] if flux is None else y[j] + cross[j] * flux)
        top = jnp.where(me == j, flux, top)
        bottom = jnp.where(me + 1 == j, flux, bottom)
    return top, bottom


def kernel(
    ns, nc, plies, classes,
    pressure_hbm, fill_hbm, class_hbm, table_hbm, span_hbm, chord_hbm, rate_hbm,
    D_c, A_c, C_c, flux_ref,
    pressure, state, table_ref, inlet_ref, rate_ref, plane_ref, half, keep_s, keep_c, A_s, C_s, E_s, E_c, D,
    sides, near_out, near_in, cross_out, cross_in, coef_s, coef_c, edge_s, edge_c,
    sent, landed,
):
    rows, width = pressure.shape[1:]
    me_s, me_c = lax.axis_index("span"), lax.axis_index("chord")
    odd = lax.rem(me_c, 2)
    beside = me_c + 1 - 2 * odd
    across = lax.rem(me_c + nc - 1 + 2 * odd, nc)
    is_odd = odd == 1
    has_across = jnp.where(is_odd, me_c < nc - 1, me_c > 0)
    lane_beside = (1 - odd) * (width - 1)
    lane_across = odd * (width - 1)

    barrier = pltpu.get_barrier_semaphore()
    loads = [
        pltpu.make_async_copy(src, dst, sent.at[i])
        for src, dst, i in (
            (span_hbm, inlet_ref.at[0], 3), (chord_hbm, inlet_ref.at[1], 3), (rate_hbm, rate_ref, 4),
            (table_hbm, table_ref, 2), (class_hbm, state.at[0], 0), (fill_hbm, state.at[1], 0),
            (pressure_hbm, pressure, 1),
        )
    ]
    for load in loads:
        load.start()
    for o in range(1, nc):
        pl.semaphore_signal(
            barrier, inc=1, device_id={"chord": lax.rem(me_c + o, nc)}, device_id_type=MESH
        )
    for to in others(ns, me_s):
        pl.semaphore_signal(barrier, inc=1, device_id={"span": to}, device_id_type=MESH)
        pl.semaphore_signal(
            barrier, inc=1, device_id={"span": to, "chord": across}, device_id_type=MESH
        )

    pltpu.make_async_copy(inlet_ref, inlet_ref, sent.at[3]).wait()
    loads[2].wait()
    row_id = lax.broadcasted_iota(jnp.int32, (rows, rate_ref.shape[1]), 0) + me_s * rows
    col_id = lax.broadcasted_iota(jnp.int32, (width, rate_ref.shape[1]), 0) + me_c * width
    row_hits = jnp.where(row_id == inlet_ref[0], rate_ref[...], 0.0)
    col_hits = jnp.where(col_id == inlet_ref[1], 1.0, 0.0)
    plane_ref[...] = lax.dot_general(
        row_hits, col_hits, (((1,), (1,)), ((), ())),
        precision=lax.Precision.HIGHEST, preferred_element_type=jnp.float32,
    )
    loads[3].wait()
    pltpu.make_async_copy(state, state, sent.at[0]).wait()
    pltpu.make_async_copy(pressure, pressure, sent.at[1]).wait()

    conds, turned, fields = [], [], []
    for p in range(plies):
        perm = jnp.full((rows, width), table_ref[p, 0], jnp.float32)
        kl = state[0, p]
        for k in range(1, classes):
            perm = jnp.where(kl == k, table_ref[p, k], perm)
        st = state[1, p]
        cond = perm * jnp.where(st == 0, 1.0, jnp.where(st == 1, 0.5, 0.25))
        conds.append(cond)
        turned.append(cond.T)
        fields.append(pressure[p].T)
        for q, v in ((p, turned[p]), (plies + p, fields[p])):
            head, tail = v[:1], v[width - 1 :]
            near_out[q : q + 1, :] = jnp.where(is_odd, head, tail)
            cross_out[q : q + 1, :] = jnp.where(is_odd, tail, head)
    pl.semaphore_wait(barrier, 2 * (ns - 1) + nc - 1)
    near = pltpu.make_async_remote_copy(
        near_out, near_in, sent.at[0], landed.at[0], {"chord": beside}, MESH
    )
    near.start()
    mine = pltpu.make_async_remote_copy(
        cross_out, cross_in.at[me_s], sent.at[1], landed.at[1], {"chord": across}, MESH
    )
    mine.start()
    for to in others(ns, me_s):
        pltpu.make_async_remote_copy(
            cross_out, cross_in.at[me_s], sent.at[1], landed.at[2], {"span": to, "chord": across}, MESH
        ).start()

    def keeper(ref, p):
        def keep(k, al, be):
            ref[k, 0, p] = al
            ref[k, 1, p] = be

        return keep

    def kept(ref, p):
        return lambda k: (ref[k, 0, p], ref[k, 1, p])

    def put(q, p, v):
        coef_s[me_s, q * plies + p : q * plies + p + 1, :] = v

    for p in range(plies):
        A, C, re = factor(conds[p], keeper(keep_s, p))
        A_s[p], C_s[p], E_s[p] = A, C, re
        put_coefs(coef_s, me_s, plies, p, A, C, conds[p])
        put(5, p, cross_out[p : p + 1, :])
        put(6, p, cross_out[plies + p : plies + p + 1, :])
        for q, response in enumerate((A.T, C.T)):
            head, tail = response[:1], response[width - 1 :]
            put(7 + q, p, jnp.where(is_odd, tail, head))
            sides[q, p : p + 1, :] = jnp.where(is_odd, head, tail)
    span_coefs = Gather("span", ns, me_s, coef_s, sent.at[2], landed.at[3])
    span_coefs.start()

    plane = plane_ref[...]
    for p in range(plies):
        f, other = fields[p], fields[plies - 1 - p]
        g = HALF_RATE * (turned[p] + up(turned[p], 1))
        flow = to_row(1, g * (up(f, 1) - f), jnp.zeros_like(f))
        back = from_row(1, down(flow, 1), jnp.zeros_like(f))
        rhs = (f + (flow - back) + COUPLE * (other - f)).T + plane
        half[p] = rhs
        edge_s[me_s, p : p + 1, :] = jnp.sum(A_s[p] * rhs, axis=0, keepdims=True)
        edge_s[me_s, plies + p : plies + p + 1, :] = jnp.sum(C_s[p] * rhs, axis=0, keepdims=True)
    near.wait_recv()
    near.wait_send()

    def inflow(ours, theirs):
        return (
            HALF_RATE
            * (theirs[:plies] + ours[:plies])
            * (theirs[plies : 2 * plies] - ours[plies : 2 * plies])
        )

    lane = lax.broadcasted_iota(jnp.int32, (plies, width), 1)
    from_beside = inflow(near_out[...], near_in[...])
    for q in range(2):
        change = jnp.sum(sides[q] * from_beside, axis=1, keepdims=True)
        edge_s[me_s, q * plies : (q + 1) * plies, :] = (
            edge_s[me_s, q * plies : (q + 1) * plies, :] + jnp.where(lane == lane_beside, change, 0.0)
        )
    span_edges = Gather("span", ns, me_s, edge_s, sent.at[3], landed.at[4])
    span_edges.start()

    for p in range(plies):
        A, C, re = factor(turned[p], keeper(keep_c, p))
        A_c[p], C_c[p], E_c[p] = A, C, re
        put_coefs(coef_c, me_c, plies, p, A, C, turned[p])
    chord_coefs = Gather("chord", nc, me_c, coef_c, sent.at[4], landed.at[5])
    chord_coefs.start()

    mine.wait_recv()
    from_across = jnp.where(has_across, inflow(cross_out[...], cross_in[me_s]), 0.0)
    lanes = lax.broadcasted_iota(jnp.int32, (width, rows), 0)
    for p in range(plies):
        change = jnp.where(lanes == lane_beside, from_beside[p : p + 1], 0.0) + jnp.where(
            lanes == lane_across, from_across[p : p + 1], 0.0
        )
        rhs = half[p] + change.T
        half[p] = rhs
        D[p] = reduce_rhs(rhs, kept(keep_s, p), E_s[p])

    few = cross_in.at[pl.ds(0, ns - 1)]
    pltpu.make_async_remote_copy(few, few, sent.at[1], landed.at[2], {"chord": across}, MESH).wait_recv()
    span_coefs.wait()
    parts = flux_factor(coef_s, ns, plies)
    by_first, by_last = [], []
    for i in range(ns):
        ours = coef_s[i, 5 * plies : 7 * plies, :]
        flow = jnp.where(has_across, inflow(ours, cross_in[i]), 0.0)
        by_first.append(jnp.sum(coef_s[i, 7 * plies : 8 * plies, :] * flow, axis=1, keepdims=True))
        by_last.append(jnp.sum(coef_s[i, 8 * plies : 9 * plies, :] * flow, axis=1, keepdims=True))
    fix = [None] + [
        jnp.where(lane == lane_across, by_last[i - 1] - by_first[i], 0.0) for i in range(1, ns)
    ]
    span_edges.wait()
    top, bottom = flux_solve(edge_s, ns, plies, me_s, *parts, fix)
    plane = plane_ref[...]
    stars = [D[p] + A_s[p] * top[p : p + 1] - C_s[p] * bottom[p : p + 1] for p in range(plies)]
    seconds = []
    for p in range(plies):
        star, other = stars[p], stars[plies - 1 - p]
        second = (2.0 * star - half[p] + COUPLE * (other - star) + plane).T
        seconds.append(second)
        edge_c[me_c, p : p + 1, :] = jnp.sum(A_c[p] * second, axis=0, keepdims=True)
        edge_c[me_c, plies + p : plies + p + 1, :] = jnp.sum(C_c[p] * second, axis=0, keepdims=True)
    chord_edges = Gather("chord", nc, me_c, edge_c, sent.at[0], landed.at[6])
    chord_edges.start()
    for p in range(plies):
        D_c[p] = reduce_rhs(seconds[p], kept(keep_c, p), E_c[p])

    chord_coefs.wait()
    parts = flux_factor(coef_c, nc, plies)
    pltpu.make_async_remote_copy(cross_in, cross_in, sent.at[1], landed.at[2], {"chord": across}, MESH).wait_send()
    for gather in (span_coefs, chord_coefs, span_edges):
        gather.wait_sent()
    chord_edges.wait()
    flux_ref[0], flux_ref[1] = flux_solve(edge_c, nc, plies, me_c, *parts)
    chord_edges.wait_sent()


def finish(plies, D_c, A_c, C_c, flux_ref, out_hbm, block, sem):
    for p in range(plies):
        top, bottom = flux_ref[0, p : p + 1, :], flux_ref[1, p : p + 1, :]
        block[p] = (D_c[p] + A_c[p] * top - C_c[p] * bottom).T
        pltpu.make_async_copy(block.at[p], out_hbm.at[p], sem.at[0]).start()
    pltpu.make_async_copy(block, out_hbm, sem.at[0]).wait()


def levels(n):
    return max(1, (n - 1).bit_length())


def per_device(ns, nc, pressure, fill_state, perm_class, perm_table, inlet_span, inlet_chord, inlet_rate):
    plies, rows, width = pressure.shape
    classes = perm_table.shape[1]
    inlets = inlet_span.shape[0]
    vmem = pl.BlockSpec(memory_space=pltpu.VMEM)
    hbm = pl.BlockSpec(memory_space=pltpu.HBM)
    f32 = jnp.float32
    block = pltpu.VMEM((plies, rows, width), f32)
    block_t = pltpu.VMEM((plies, width, rows), f32)
    dma = lambda n: pltpu.SemaphoreType.DMA((n,))
    lines = pltpu.VMEM((plies, width, rows), f32)
    solved = pl.pallas_call(
        functools.partial(kernel, ns, nc, plies, classes),
        out_shape=(lines, lines, lines, pltpu.VMEM((2, plies, rows), f32)),
        in_specs=[hbm] * 7,
        out_specs=(vmem,) * 4,
        scratch_shapes=[
            block, pltpu.VMEM((2, plies, rows, width), jnp.int32),
            pltpu.SMEM(perm_table.shape, f32),
            pltpu.VMEM((2, 1, inlets), jnp.int32), pltpu.VMEM((1, inlets), f32),
            pltpu.VMEM((rows, width), f32),
            block,
            pltpu.VMEM((levels(rows), 2, plies, rows, width), f32),
            pltpu.VMEM((levels(width), 2, plies, width, rows), f32),
            block, block, block, block_t, block,
            pltpu.VMEM((2, plies, rows), f32),
            pltpu.VMEM((2 * plies, rows), f32),
            pltpu.VMEM((2 * plies, rows), f32),
            pltpu.VMEM((2 * plies, rows), f32),
            pltpu.VMEM((ns, 2 * plies, rows), f32),
            pltpu.VMEM((ns, 9 * plies, width), f32),
            pltpu.VMEM((nc, 5 * plies, rows), f32),
            pltpu.VMEM((ns, 2 * plies, width), f32),
            pltpu.VMEM((nc, 2 * plies, rows), f32),
            dma(5), dma(7),
        ],
        compiler_params=pltpu.CompilerParams(collective_id=0, has_side_effects=True, vmem_limit_bytes=LIMIT),
    )(
        *(
            pltpu.with_memory_space_constraint(x, pltpu.HBM)
            for x in (
                pressure, fill_state, perm_class, perm_table, inlet_span.reshape(1, inlets),
                inlet_chord.reshape(1, inlets), inlet_rate.reshape(1, inlets),
            )
        )
    )
    return pl.pallas_call(
        functools.partial(finish, plies),
        out_shape=jax.ShapeDtypeStruct(pressure.shape, f32),
        in_specs=[vmem] * 4,
        out_specs=hbm,
        scratch_shapes=[block, dma(1)],
        compiler_params=pltpu.CompilerParams(vmem_limit_bytes=LIMIT),
    )(*solved)


def solution(mesh):
    block = P(None, "span", "chord")
    return jax.shard_map(
        functools.partial(per_device, mesh.shape["span"], mesh.shape["chord"]),
        mesh=mesh,
        in_specs=(block, block, block, P(), P(), P(), P()),
        out_specs=block,
        check_vma=False,
    )
```

time: 15.1 us -> 14.7 us (0.974)
  Pallas kernels: 14.9 us -> 14.5 us
    pallas_call x1, Pallas kernels: 14.1 us -> 13.8 us  [per_device(): pl.pallas_call(functools.partial(kernel, ns, nc, plies, classes), out_sha...]
where the time goes in v2:
time: 14.7 us; the launch traced here: 14.6 us
  Pallas kernels  14.5 us (99%)
    pallas_call x1, Pallas kernels, per_device(): pl.pallas_call(functools.partial(kernel, ns, nc, plies, classes), out_sha...  13.8 us
    pallas_call x1, Pallas kernels, per_device(): pl.pallas_call(functools.partial(finish, plies), out_shape=jax.ShapeDtype...  0.77 us

profile of v2, /device:TPU:0, one launch (start us, length us, event | category | flops | bytes accessed | tf_op | source)
XLA Modules:
  0.0 14.6 jit_solution(1685041713756959080)
XLA Ops:
  0.0 13.8 %shard_map.73 = (f32[2,128,128]{2,1,0:T(8,128)S(1)}, f32[2,128,128]{2,1,0:T(8,128)S(1)}, f32[2,128,128]{2,1,0:T(8,128)S(1)}, f32[2,2,128]{2,1,0:T(2,128)S(1)}) custom-call(f32[2,128,128]{2,1,0:T(8,128)} %pressure_hbm.1, s32[2,128,128]{2,1,0:T(8,128)} %fill_hbm.1, s32[2,128,128]{2,1,0:T(8,128)} %class_hbm.1, f32[2,8]{1,0:T(2,128)} %table_hbm.1, ...), custom_call_target="tpu_custom_call" | custom-call | tf_op jit(solution)/shard_map/pallas_call | solution.py:368
  13.8 0.8 %shard_map.74 = f32[2,128,128]{2,1,0:T(8,128)} custom-call(f32[2,128,128]{2,1,0:T(8,128)S(1)} %get-tuple-element.9.D_c, f32[2,128,128]{2,1,0:T(8,128)S(1)} %get-tuple-element.10.A_c, f32[2,128,128]{2,1,0:T(8,128)S(1)} %get-tuple-element.11.C_c, f32[2,2,128]{2,1,0:T(2,128)S(1)} %get-tuple-element.12.flux_ref), custom_call_target="tpu_custom_call" | custom-call | tf_op jit(solution)/shard_map/pallas_call | solution.py:403

commit v3 on v2

--- a/solution.py
+++ b/solution.py
@@ -108,21 +108,25 @@
         self.all.wait_send()
 
 
-def put_coefs(buf, me, plies, p, A, C, cond):
+def put(buf, me, plies, q, p, v):
+    buf[me, q * plies + p : q * plies + p + 1, :] = v
+
+
+def put_responses(buf, me, plies, p, A, C):
     n = A.shape[0]
-    values = (A[:1], C[n - 1 :], A[n - 1 :], cond[:1], cond[n - 1 :])
-    for q, v in enumerate(values):
-        buf[me, q * plies + p : q * plies + p + 1, :] = v
-
-
-def flux_factor(buf, n, plies):
-    def at(j, q):
+    for q, v in enumerate((A[:1], C[n - 1 :], A[n - 1 :])):
+        put(buf, me, plies, q, p, v)
+
+
+def flux_factor(ends, responses, n, plies):
+    def of(buf, j, q):
         return buf[j, q * plies : (q + 1) * plies, :]
 
     w, m = [None] * (n + 1), [None] * (n + 1)
-    cross = [at(j, 2) for j in range(n)]
+    cross = [of(responses, j, 2) for j in range(n)]
     for j in range(1, n):
-        diag = 1.0 / (HALF_RATE * (at(j - 1, 4) + at(j, 3))) + at(j - 1, 1) + at(j, 0)
+        diag = 1.0 / (HALF_RATE * (of(ends, j - 1, 1) + of(ends, j, 0)))
+        diag = diag + of(responses, j - 1, 1) + of(responses, j, 0)
         if j > 1:
             m[j] = cross[j - 1] * w[j - 1]
             diag = diag - cross[j - 1] * m[j]
@@ -152,7 +156,7 @@
     pressure_hbm, fill_hbm, class_hbm, table_hbm, span_hbm, chord_hbm, rate_hbm,
     D_c, A_c, C_c, flux_ref,
     pressure, state, table_ref, inlet_ref, rate_ref, plane_ref, half, keep_s, keep_c, A_s, C_s, E_s, E_c, D,
-    sides, near_out, near_in, cross_out, cross_in, coef_s, coef_c, edge_s, edge_c,
+    sides, near_out, near_in, cross_out, cross_in, ends_s, coef_s, coef_c, edge_c,
     sent, landed,
 ):
     rows, width = pressure.shape[1:]
@@ -215,6 +219,9 @@
             head, tail = v[:1], v[width - 1 :]
             near_out[q : q + 1, :] = jnp.where(is_odd, head, tail)
             cross_out[q : q + 1, :] = jnp.where(is_odd, tail, head)
+            ends_s[me_s, 2 * plies + q : 2 * plies + q + 1, :] = jnp.where(is_odd, tail, head)
+        for q, v in enumerate((cond[:1], cond[rows - 1 :])):
+            put(ends_s, me_s, plies, q, p, v)
     pl.semaphore_wait(barrier, 2 * (ns - 1) + nc - 1)
     near = pltpu.make_async_remote_copy(
         near_out, near_in, sent.at[0], landed.at[0], {"chord": beside}, MESH
@@ -228,6 +235,8 @@
         pltpu.make_async_remote_copy(
             cross_out, cross_in.at[me_s], sent.at[1], landed.at[2], {"span": to, "chord": across}, MESH
         ).start()
+    span_ends = Gather("span", ns, me_s, ends_s, sent.at[3], landed.at[4])
+    span_ends.start()
 
     def keeper(ref, p):
         def keep(k, al, be):
@@ -239,21 +248,14 @@
     def kept(ref, p):
         return lambda k: (ref[k, 0, p], ref[k, 1, p])
 
-    def put(q, p, v):
-        coef_s[me_s, q * plies + p : q * plies + p + 1, :] = v
-
     for p in range(plies):
         A, C, re = factor(conds[p], keeper(keep_s, p))
         A_s[p], C_s[p], E_s[p] = A, C, re
-        put_coefs(coef_s, me_s, plies, p, A, C, conds[p])
-        put(5, p, cross_out[p : p + 1, :])
-        put(6, p, cross_out[plies + p : plies + p + 1, :])
+        put_responses(coef_s, me_s, plies, p, A, C)
         for q, response in enumerate((A.T, C.T)):
             head, tail = response[:1], response[width - 1 :]
-            put(7 + q, p, jnp.where(is_odd, tail, head))
+            put(coef_s, me_s, plies, 3 + q, p, jnp.where(is_odd, tail, head))
             sides[q, p : p + 1, :] = jnp.where(is_odd, head, tail)
-    span_coefs = Gather("span", ns, me_s, coef_s, sent.at[2], landed.at[3])
-    span_coefs.start()
 
     plane = plane_ref[...]
     for p in range(plies):
@@ -263,8 +265,8 @@
         back = from_row(1, down(flow, 1), jnp.zeros_like(f))
         rhs = (f + (flow - back) + COUPLE * (other - f)).T + plane
         half[p] = rhs
-        edge_s[me_s, p : p + 1, :] = jnp.sum(A_s[p] * rhs, axis=0, keepdims=True)
-        edge_s[me_s, plies + p : plies + p + 1, :] = jnp.sum(C_s[p] * rhs, axis=0, keepdims=True)
+        put(coef_s, me_s, plies, 5, p, jnp.sum(A_s[p] * rhs, axis=0, keepdims=True))
+        put(coef_s, me_s, plies, 6, p, jnp.sum(C_s[p] * rhs, axis=0, keepdims=True))
     near.wait_recv()
     near.wait_send()
 
@@ -279,16 +281,26 @@
     from_beside = inflow(near_out[...], near_in[...])
     for q in range(2):
         change = jnp.sum(sides[q] * from_beside, axis=1, keepdims=True)
-        edge_s[me_s, q * plies : (q + 1) * plies, :] = (
-            edge_s[me_s, q * plies : (q + 1) * plies, :] + jnp.where(lane == lane_beside, change, 0.0)
-        )
-    span_edges = Gather("span", ns, me_s, edge_s, sent.at[3], landed.at[4])
-    span_edges.start()
-
-    for p in range(plies):
-        A, C, re = factor(turned[p], keeper(keep_c, p))
-        A_c[p], C_c[p], E_c[p] = A, C, re
-        put_coefs(coef_c, me_c, plies, p, A, C, turned[p])
+        coef_s[me_s, (5 + q) * plies : (6 + q) * plies, :] = (
+            coef_s[me_s, (5 + q) * plies : (6 + q) * plies, :]
+            + jnp.where(lane == lane_beside, change, 0.0)
+        )
+    span_coefs = Gather("span", ns, me_s, coef_s, sent.at[2], landed.at[3])
+    span_coefs.start()
+
+    for p in range(plies):
+        A_c[p] = turned[p]
+
+    @pl.when(me_c >= 0)
+    def after_sending_span():
+        for p in range(plies):
+            cond = A_c[p]
+            put(coef_c, me_c, plies, 3, p, cond[:1])
+            put(coef_c, me_c, plies, 4, p, cond[width - 1 :])
+            A, C, re = factor(cond, keeper(keep_c, p))
+            A_c[p], C_c[p], E_c[p] = A, C, re
+            put_responses(coef_c, me_c, plies, p, A, C)
+
     chord_coefs = Gather("chord", nc, me_c, coef_c, sent.at[4], landed.at[5])
     chord_coefs.start()
 
@@ -305,37 +317,39 @@
 
     few = cross_in.at[pl.ds(0, ns - 1)]
     pltpu.make_async_remote_copy(few, few, sent.at[1], landed.at[2], {"chord": across}, MESH).wait_recv()
+    span_ends.wait()
     span_coefs.wait()
-    parts = flux_factor(coef_s, ns, plies)
+    parts = flux_factor(ends_s, coef_s, ns, plies)
     by_first, by_last = [], []
     for i in range(ns):
-        ours = coef_s[i, 5 * plies : 7 * plies, :]
+        ours = ends_s[i, 2 * plies : 4 * plies, :]
         flow = jnp.where(has_across, inflow(ours, cross_in[i]), 0.0)
-        by_first.append(jnp.sum(coef_s[i, 7 * plies : 8 * plies, :] * flow, axis=1, keepdims=True))
-        by_last.append(jnp.sum(coef_s[i, 8 * plies : 9 * plies, :] * flow, axis=1, keepdims=True))
+        by_first.append(jnp.sum(coef_s[i, 3 * plies : 4 * plies, :] * flow, axis=1, keepdims=True))
+        by_last.append(jnp.sum(coef_s[i, 4 * plies : 5 * plies, :] * flow, axis=1, keepdims=True))
     fix = [None] + [
         jnp.where(lane == lane_across, by_last[i - 1] - by_first[i], 0.0) for i in range(1, ns)
     ]
-    span_edges.wait()
-    top, bottom = flux_solve(edge_s, ns, plies, me_s, *parts, fix)
+    top, bottom = flux_solve(coef_s.at[:, pl.ds(5 * plies, 2 * plies)], ns, plies, me_s, *parts, fix)
     plane = plane_ref[...]
     stars = [D[p] + A_s[p] * top[p : p + 1] - C_s[p] * bottom[p : p + 1] for p in range(plies)]
-    seconds = []
     for p in range(plies):
         star, other = stars[p], stars[plies - 1 - p]
         second = (2.0 * star - half[p] + COUPLE * (other - star) + plane).T
-        seconds.append(second)
+        D_c[p] = second
         edge_c[me_c, p : p + 1, :] = jnp.sum(A_c[p] * second, axis=0, keepdims=True)
         edge_c[me_c, plies + p : plies + p + 1, :] = jnp.sum(C_c[p] * second, axis=0, keepdims=True)
     chord_edges = Gather("chord", nc, me_c, edge_c, sent.at[0], landed.at[6])
     chord_edges.start()
-    for p in range(plies):
-        D_c[p] = reduce_rhs(seconds[p], kept(keep_c, p), E_c[p])
+
+    @pl.when(me_c >= 0)
+    def after_sending():
+        for p in range(plies):
+            D_c[p] = reduce_rhs(D_c[p], kept(keep_c, p), E_c[p])
 
     chord_coefs.wait()
-    parts = flux_factor(coef_c, nc, plies)
+    parts = flux_factor(coef_c.at[:, pl.ds(3 * plies, 2 * plies)], coef_c, nc, plies)
     pltpu.make_async_remote_copy(cross_in, cross_in, sent.at[1], landed.at[2], {"chord": across}, MESH).wait_send()
-    for gather in (span_coefs, chord_coefs, span_edges):
+    for gather in (span_ends, span_coefs, chord_coefs):
         gather.wait_sent()
     chord_edges.wait()
     flux_ref[0], flux_ref[1] = flux_solve(edge_c, nc, plies, me_c, *parts)
@@ -384,9 +398,9 @@
             pltpu.VMEM((2 * plies, rows), f32),
             pltpu.VMEM((2 * plies, rows), f32),
             pltpu.VMEM((ns, 2 * plies, rows), f32),
-            pltpu.VMEM((ns, 9 * plies, width), f32),
+            pltpu.VMEM((ns, 4 * plies, width), f32),
+            pltpu.VMEM((ns, 7 * plies, width), f32),
             pltpu.VMEM((nc, 5 * plies, rows), f32),
-            pltpu.VMEM((ns, 2 * plies, width), f32),
             pltpu.VMEM((nc, 2 * plies, rows), f32),
             dma(5), dma(7),
         ],

time: 14.7 us -> 14.3 us (0.973)
  Pallas kernels: 14.5 us -> 14.1 us
    pallas_call x1, Pallas kernels: 13.8 us -> 13.3 us  [per_device(): pl.pallas_call(functools.partial(kernel, ns, nc, plies, classes), out_sha...]
where the time goes in v3:
time: 14.3 us; the launch traced here: 14.1 us
  Pallas kernels  14.1 us (99%)
    pallas_call x1, Pallas kernels, per_device(): pl.pallas_call(functools.partial(kernel, ns, nc, plies, classes), out_sha...  13.3 us
    pallas_call x1, Pallas kernels, per_device(): pl.pallas_call(functools.partial(finish, plies), out_shape=jax.ShapeDtype...  0.77 us

profile of v3, /device:TPU:0, one launch (start us, length us, event | category | flops | bytes accessed | tf_op | source)
XLA Modules:
  0.0 14.1 jit_solution(12645077297793411115)
XLA Ops:
  0.0 13.3 %shard_map.73 = (f32[2,128,128]{2,1,0:T(8,128)S(1)}, f32[2,128,128]{2,1,0:T(8,128)S(1)}, f32[2,128,128]{2,1,0:T(8,128)S(1)}, f32[2,2,128]{2,1,0:T(2,128)S(1)}) custom-call(f32[2,128,128]{2,1,0:T(8,128)} %pressure_hbm.1, s32[2,128,128]{2,1,0:T(8,128)} %fill_hbm.1, s32[2,128,128]{2,1,0:T(8,128)} %class_hbm.1, f32[2,8]{1,0:T(2,128)} %table_hbm.1, ...), custom_call_target="tpu_custom_call" | custom-call | tf_op jit(solution)/shard_map/pallas_call | solution.py:382
  13.4 0.8 %shard_map.74 = f32[2,128,128]{2,1,0:T(8,128)} custom-call(f32[2,128,128]{2,1,0:T(8,128)S(1)} %get-tuple-element.9.D_c, f32[2,128,128]{2,1,0:T(8,128)S(1)} %get-tuple-element.10.A_c, f32[2,128,128]{2,1,0:T(8,128)S(1)} %get-tuple-element.11.C_c, f32[2,2,128]{2,1,0:T(2,128)S(1)} %get-tuple-element.12.flux_ref), custom_call_target="tpu_custom_call" | custom-call | tf_op jit(solution)/shard_map/pallas_call | solution.py:417

commit v4 on v3

--- a/solution.py
+++ b/solution.py
@@ -41,14 +41,13 @@
     return jnp.where(rows < n - s, value, other)
 
 
-def factor(cond, keep):
-    n = cond.shape[0]
-    zero = jnp.zeros_like(cond)
-    one = jnp.ones_like(cond)
-    g = HALF_RATE * (cond + up(cond, 1))
-    a = from_row(1, down(g, 1), one)
-    c = to_row(1, g, one)
-    e = one
+def faces(cond):
+    return to_row(1, HALF_RATE * (cond + up(cond, 1)), jnp.zeros_like(cond))
+
+
+def eliminate(a, c, e, keep):
+    n = e.shape[0]
+    zero = jnp.zeros_like(e)
     s, k = 1, 0
     while s < n:
         a_in = from_row(s, a, zero)
@@ -63,6 +62,64 @@
         s, k = 2 * s, k + 1
     re = 1.0 / e
     return a * re, c * re, re
+
+
+def factor(cond, keep):
+    one = jnp.ones_like(cond)
+    g = HALF_RATE * (cond + up(cond, 1))
+    return eliminate(from_row(1, down(g, 1), one), to_row(1, g, one), one, keep)
+
+
+def responses(conds, g_ref, e_ref, A_ref, C_ref):
+    n, w = conds[0].shape
+    count = len(conds)
+    top = [jnp.ones((1, w), jnp.float32)] * count
+    g_now, e_now = [faces(cond) for cond in conds], None
+    steps = []
+    while n > TILE:
+        m = n // 2
+        step = []
+        for p in range(count):
+            g_ref[p, :n, :] = g_now[p]
+            if e_now is not None:
+                e_ref[p, :n, :] = e_now[p]
+        for p in range(count):
+            g_even, g_odd = g_ref[p, pl.ds(0, m, 2), :], g_ref[p, pl.ds(1, m, 2), :]
+            if e_now is None:
+                e_even, e_odd = jnp.ones((m, w), jnp.float32), jnp.ones((m, w), jnp.float32)
+            else:
+                e_even, e_odd = e_ref[p, pl.ds(0, m, 2), :], e_ref[p, pl.ds(1, m, 2), :]
+            before = down(g_odd, 1)
+            zero = jnp.zeros_like(before)
+            a = from_row(1, before, zero)
+            rb = 1.0 / (e_even + a + g_even)
+            P = from_row(1, before, jnp.broadcast_to(top[p], before.shape)) * rb
+            Q = g_even * rb
+            step.append((P, Q))
+            top[p] = Q[:1] * top[p]
+            g_now[p] = to_row(1, up(P * g_even, 1), zero)
+            e_new = e_odd + Q * e_even + to_row(1, up(P * e_even, 1), zero)
+            step[p] = (P, Q, e_new)
+        e_now = [x[2] for x in step]
+        steps.append((m, step))
+        n = m
+    lines = []
+    for p in range(count):
+        one = jnp.ones((n, w), jnp.float32)
+        e = one if e_now is None else e_now[p]
+        a = from_row(1, down(g_now[p], 1), jnp.broadcast_to(top[p], e.shape))
+        lines.append(eliminate(a, to_row(1, g_now[p], one), e, lambda *x: None)[:2])
+    for m, step in reversed(steps):
+        for p in range(count):
+            P, Q, _ = step[p]
+            first, last = lines[p]
+            A_ref[p, pl.ds(1, m, 2), :] = first
+            C_ref[p, pl.ds(1, m, 2), :] = last
+            A_ref[p, pl.ds(0, m, 2), :] = P * from_row(1, down(first, 1), jnp.ones_like(first)) + Q * first
+            C_ref[p, pl.ds(0, m, 2), :] = P * from_row(1, down(last, 1), jnp.zeros_like(last)) + Q * last
+        for p in range(count):
+            lines[p] = (A_ref[p, : 2 * m, :], C_ref[p, : 2 * m, :])
+    return lines
 
 
 def reduce_rhs(d, kept, re):
@@ -155,7 +212,7 @@
     ns, nc, plies, classes,
     pressure_hbm, fill_hbm, class_hbm, table_hbm, span_hbm, chord_hbm, rate_hbm,
     D_c, A_c, C_c, flux_ref,
-    pressure, state, table_ref, inlet_ref, rate_ref, plane_ref, half, keep_s, keep_c, A_s, C_s, E_s, E_c, D,
+    pressure, state, table_ref, inlet_ref, rate_ref, plane_ref, half, keep_s, keep_c, g_ref, e_ref, A_s, C_s, E_s, E_c, D,
     sides, near_out, near_in, cross_out, cross_in, ends_s, coef_s, coef_c, edge_c,
     sent, landed,
 ):
@@ -248,9 +305,7 @@
     def kept(ref, p):
         return lambda k: (ref[k, 0, p], ref[k, 1, p])
 
-    for p in range(plies):
-        A, C, re = factor(conds[p], keeper(keep_s, p))
-        A_s[p], C_s[p], E_s[p] = A, C, re
+    for p, (A, C) in enumerate(responses(conds, g_ref, e_ref, A_s, C_s)):
         put_responses(coef_s, me_s, plies, p, A, C)
         for q, response in enumerate((A.T, C.T)):
             head, tail = response[:1], response[width - 1 :]
@@ -268,7 +323,6 @@
         put(coef_s, me_s, plies, 5, p, jnp.sum(A_s[p] * rhs, axis=0, keepdims=True))
         put(coef_s, me_s, plies, 6, p, jnp.sum(C_s[p] * rhs, axis=0, keepdims=True))
     near.wait_recv()
-    near.wait_send()
 
     def inflow(ours, theirs):
         return (
@@ -290,9 +344,12 @@
 
     for p in range(plies):
         A_c[p] = turned[p]
+        D[p] = conds[p]
 
     @pl.when(me_c >= 0)
     def after_sending_span():
+        for p in range(plies):
+            E_s[p] = factor(D[p], keeper(keep_s, p))[2]
         for p in range(plies):
             cond = A_c[p]
             put(coef_c, me_c, plies, 3, p, cond[:1])
@@ -304,6 +361,7 @@
     chord_coefs = Gather("chord", nc, me_c, coef_c, sent.at[4], landed.at[5])
     chord_coefs.start()
 
+    near.wait_send()
     mine.wait_recv()
     from_across = jnp.where(has_across, inflow(cross_out[...], cross_in[me_s]), 0.0)
     lanes = lax.broadcasted_iota(jnp.int32, (width, rows), 0)
@@ -392,6 +450,7 @@
             block,
             pltpu.VMEM((levels(rows), 2, plies, rows, width), f32),
             pltpu.VMEM((levels(width), 2, plies, width, rows), f32),
+            block, block,
             block, block, block, block_t, block,
             pltpu.VMEM((2, plies, rows), f32),
             pltpu.VMEM((2 * plies, rows), f32),

time: 14.3 us -> 13.9 us (0.972)
  Pallas kernels: 14.1 us -> 13.7 us
    pallas_call x1, Pallas kernels: 13.3 us -> 13 us  [per_device(): pl.pallas_call(functools.partial(kernel, ns, nc, plies, classes), out_sha...]
where the time goes in v4:
time: 13.9 us; the launch traced here: 13.7 us
  Pallas kernels  13.7 us (99%)
    pallas_call x1, Pallas kernels, per_device(): pl.pallas_call(functools.partial(kernel, ns, nc, plies, classes), out_sha...  13 us
    pallas_call x1, Pallas kernels, per_device(): pl.pallas_call(functools.partial(finish, plies), out_shape=jax.ShapeDtype...  0.77 us

profile of v4, /device:TPU:0, one launch (start us, length us, event | category | flops | bytes accessed | tf_op | source)
XLA Modules:
  0.0 13.7 jit_solution(9756706699333299760)
XLA Ops:
  0.0 13.0 %shard_map.73 = (f32[2,128,128]{2,1,0:T(8,128)S(1)}, f32[2,128,128]{2,1,0:T(8,128)S(1)}, f32[2,128,128]{2,1,0:T(8,128)S(1)}, f32[2,2,128]{2,1,0:T(2,128)S(1)}) custom-call(f32[2,128,128]{2,1,0:T(8,128)} %pressure_hbm.1, s32[2,128,128]{2,1,0:T(8,128)} %fill_hbm.1, s32[2,128,128]{2,1,0:T(8,128)} %class_hbm.1, f32[2,8]{1,0:T(2,128)} %table_hbm.1, ...), custom_call_target="tpu_custom_call" | custom-call | tf_op jit(solution)/shard_map/pallas_call | solution.py:440
  13.0 0.8 %shard_map.74 = f32[2,128,128]{2,1,0:T(8,128)} custom-call(f32[2,128,128]{2,1,0:T(8,128)S(1)} %get-tuple-element.9.D_c, f32[2,128,128]{2,1,0:T(8,128)S(1)} %get-tuple-element.10.A_c, f32[2,128,128]{2,1,0:T(8,128)S(1)} %get-tuple-element.11.C_c, f32[2,2,128]{2,1,0:T(2,128)S(1)} %get-tuple-element.12.flux_ref), custom_call_target="tpu_custom_call" | custom-call | tf_op jit(solution)/shard_map/pallas_call | solution.py:476

commit v5 on v4

--- a/solution.py
+++ b/solution.py
@@ -175,15 +175,21 @@
         put(buf, me, plies, q, p, v)
 
 
-def flux_factor(ends, responses, n, plies):
-    def of(buf, j, q):
-        return buf[j, q * plies : (q + 1) * plies, :]
-
+def of(buf, j, q, plies):
+    return buf[j, q * plies : (q + 1) * plies, :]
+
+
+def face_gaps(ends, n, plies):
+    return [None] + [
+        1.0 / (HALF_RATE * (of(ends, j - 1, 1, plies) + of(ends, j, 0, plies))) for j in range(1, n)
+    ]
+
+
+def flux_factor(gaps, responses, n, plies):
     w, m = [None] * (n + 1), [None] * (n + 1)
-    cross = [of(responses, j, 2) for j in range(n)]
+    cross = [of(responses, j, 2, plies) for j in range(n)]
     for j in range(1, n):
-        diag = 1.0 / (HALF_RATE * (of(ends, j - 1, 1) + of(ends, j, 0)))
-        diag = diag + of(responses, j - 1, 1) + of(responses, j, 0)
+        diag = gaps[j] + of(responses, j - 1, 1, plies) + of(responses, j, 0, plies)
         if j > 1:
             m[j] = cross[j - 1] * w[j - 1]
             diag = diag - cross[j - 1] * m[j]
@@ -227,14 +233,16 @@
     lane_across = odd * (width - 1)
 
     barrier = pltpu.get_barrier_semaphore()
-    loads = [
-        pltpu.make_async_copy(src, dst, sent.at[i])
-        for src, dst, i in (
-            (span_hbm, inlet_ref.at[0], 3), (chord_hbm, inlet_ref.at[1], 3), (rate_hbm, rate_ref, 4),
-            (table_hbm, table_ref, 2), (class_hbm, state.at[0], 0), (fill_hbm, state.at[1], 0),
-            (pressure_hbm, pressure, 1),
-        )
+    pairs = [
+        (span_hbm, inlet_ref.at[0], plies + 2), (chord_hbm, inlet_ref.at[1], plies + 2),
+        (rate_hbm, rate_ref, plies + 3), (table_hbm, table_ref, plies + 1),
     ]
+    for p in range(plies):
+        pairs.append((class_hbm.at[p], state.at[p, 0], p))
+        pairs.append((fill_hbm.at[p], state.at[p, 1], p))
+        if p == 0:
+            pairs.append((pressure_hbm, pressure, plies))
+    loads = [pltpu.make_async_copy(src, dst, sent.at[i]) for src, dst, i in pairs]
     for load in loads:
         load.start()
     for o in range(1, nc):
@@ -247,7 +255,7 @@
             barrier, inc=1, device_id={"span": to, "chord": across}, device_id_type=MESH
         )
 
-    pltpu.make_async_copy(inlet_ref, inlet_ref, sent.at[3]).wait()
+    pltpu.make_async_copy(inlet_ref, inlet_ref, sent.at[plies + 2]).wait()
     loads[2].wait()
     row_id = lax.broadcasted_iota(jnp.int32, (rows, rate_ref.shape[1]), 0) + me_s * rows
     col_id = lax.broadcasted_iota(jnp.int32, (width, rate_ref.shape[1]), 0) + me_c * width
@@ -258,16 +266,17 @@
         precision=lax.Precision.HIGHEST, preferred_element_type=jnp.float32,
     )
     loads[3].wait()
-    pltpu.make_async_copy(state, state, sent.at[0]).wait()
-    pltpu.make_async_copy(pressure, pressure, sent.at[1]).wait()
 
     conds, turned, fields = [], [], []
     for p in range(plies):
+        pltpu.make_async_copy(state.at[p], state.at[p], sent.at[p]).wait()
+        if p == 0:
+            loads[6].wait()
         perm = jnp.full((rows, width), table_ref[p, 0], jnp.float32)
-        kl = state[0, p]
+        kl = state[p, 0]
         for k in range(1, classes):
             perm = jnp.where(kl == k, table_ref[p, k], perm)
-        st = state[1, p]
+        st = state[p, 1]
         cond = perm * jnp.where(st == 0, 1.0, jnp.where(st == 1, 0.5, 0.25))
         conds.append(cond)
         turned.append(cond.T)
@@ -372,31 +381,37 @@
         rhs = half[p] + change.T
         half[p] = rhs
         D[p] = reduce_rhs(rhs, kept(keep_s, p), E_s[p])
+    for p in range(plies):
+        star, other = D[p], D[plies - 1 - p]
+        half[p] = 2.0 * star - half[p] + COUPLE * (other - star) + plane_ref[...]
 
     few = cross_in.at[pl.ds(0, ns - 1)]
     pltpu.make_async_remote_copy(few, few, sent.at[1], landed.at[2], {"chord": across}, MESH).wait_recv()
     span_ends.wait()
+    flows = [
+        jnp.where(has_across, inflow(ends_s[i, 2 * plies : 4 * plies, :], cross_in[i]), 0.0)
+        for i in range(ns)
+    ]
+    gaps = face_gaps(ends_s, ns, plies)
     span_coefs.wait()
-    parts = flux_factor(ends_s, coef_s, ns, plies)
+    parts = flux_factor(gaps, coef_s, ns, plies)
     by_first, by_last = [], []
     for i in range(ns):
-        ours = ends_s[i, 2 * plies : 4 * plies, :]
-        flow = jnp.where(has_across, inflow(ours, cross_in[i]), 0.0)
+        flow = flows[i]
         by_first.append(jnp.sum(coef_s[i, 3 * plies : 4 * plies, :] * flow, axis=1, keepdims=True))
         by_last.append(jnp.sum(coef_s[i, 4 * plies : 5 * plies, :] * flow, axis=1, keepdims=True))
     fix = [None] + [
         jnp.where(lane == lane_across, by_last[i - 1] - by_first[i], 0.0) for i in range(1, ns)
     ]
     top, bottom = flux_solve(coef_s.at[:, pl.ds(5 * plies, 2 * plies)], ns, plies, me_s, *parts, fix)
-    plane = plane_ref[...]
-    stars = [D[p] + A_s[p] * top[p : p + 1] - C_s[p] * bottom[p : p + 1] for p in range(plies)]
-    for p in range(plies):
-        star, other = stars[p], stars[plies - 1 - p]
-        second = (2.0 * star - half[p] + COUPLE * (other - star) + plane).T
+    gains = [A_s[p] * top[p : p + 1] - C_s[p] * bottom[p : p + 1] for p in range(plies)]
+    for p in range(plies):
+        star, other = gains[p], gains[plies - 1 - p]
+        second = (half[p] + ((2.0 - COUPLE) * star + COUPLE * other)).T
         D_c[p] = second
         edge_c[me_c, p : p + 1, :] = jnp.sum(A_c[p] * second, axis=0, keepdims=True)
         edge_c[me_c, plies + p : plies + p + 1, :] = jnp.sum(C_c[p] * second, axis=0, keepdims=True)
-    chord_edges = Gather("chord", nc, me_c, edge_c, sent.at[0], landed.at[6])
+    chord_edges = Gather("chord", nc, me_c, edge_c, sent.at[5], landed.at[6])
     chord_edges.start()
 
     @pl.when(me_c >= 0)
@@ -405,7 +420,7 @@
             D_c[p] = reduce_rhs(D_c[p], kept(keep_c, p), E_c[p])
 
     chord_coefs.wait()
-    parts = flux_factor(coef_c.at[:, pl.ds(3 * plies, 2 * plies)], coef_c, nc, plies)
+    parts = flux_factor(face_gaps(coef_c.at[:, pl.ds(3 * plies, 2 * plies)], nc, plies), coef_c, nc, plies)
     pltpu.make_async_remote_copy(cross_in, cross_in, sent.at[1], landed.at[2], {"chord": across}, MESH).wait_send()
     for gather in (span_ends, span_coefs, chord_coefs):
         gather.wait_sent()
@@ -443,7 +458,7 @@
         in_specs=[hbm] * 7,
         out_specs=(vmem,) * 4,
         scratch_shapes=[
-            block, pltpu.VMEM((2, plies, rows, width), jnp.int32),
+            block, pltpu.VMEM((plies, 2, rows, width), jnp.int32),
             pltpu.SMEM(perm_table.shape, f32),
             pltpu.VMEM((2, 1, inlets), jnp.int32), pltpu.VMEM((1, inlets), f32),
             pltpu.VMEM((rows, width), f32),
@@ -461,7 +476,7 @@
             pltpu.VMEM((ns, 7 * plies, width), f32),
             pltpu.VMEM((nc, 5 * plies, rows), f32),
             pltpu.VMEM((nc, 2 * plies, rows), f32),
-            dma(5), dma(7),
+            dma(max(6, plies + 4)), dma(7),
         ],
         compiler_params=pltpu.CompilerParams(collective_id=0, has_side_effects=True, vmem_limit_bytes=LIMIT),
     )(

time: 13.9 us -> 13.9 us (level)
  no operation moved by 1% of the time
where the time goes in v5:
time: 13.9 us; the launch traced here: 13.7 us
  Pallas kernels  13.7 us (99%)
    pallas_call x1, Pallas kernels, per_device(): pl.pallas_call(functools.partial(kernel, ns, nc, plies, classes), out_sha...  13 us
    pallas_call x1, Pallas kernels, per_device(): pl.pallas_call(functools.partial(finish, plies), out_shape=jax.ShapeDtype...  0.77 us

profile of v5, /device:TPU:0, one launch (start us, length us, event | category | flops | bytes accessed | tf_op | source)
XLA Modules:
  0.0 13.7 jit_solution(15924656967129437560)
XLA Ops:
  0.0 13.0 %shard_map.73 = (f32[2,128,128]{2,1,0:T(8,128)S(1)}, f32[2,128,128]{2,1,0:T(8,128)S(1)}, f32[2,128,128]{2,1,0:T(8,128)S(1)}, f32[2,2,128]{2,1,0:T(2,128)S(1)}) custom-call(f32[2,128,128]{2,1,0:T(8,128)} %pressure_hbm.1, s32[2,128,128]{2,1,0:T(8,128)} %fill_hbm.1, s32[2,128,128]{2,1,0:T(8,128)} %class_hbm.1, f32[2,8]{1,0:T(2,128)} %table_hbm.1, ...), custom_call_target="tpu_custom_call" | custom-call | tf_op jit(solution)/shard_map/pallas_call | solution.py:455
  13.0 0.8 %shard_map.74 = f32[2,128,128]{2,1,0:T(8,128)} custom-call(f32[2,128,128]{2,1,0:T(8,128)S(1)} %get-tuple-element.9.D_c, f32[2,128,128]{2,1,0:T(8,128)S(1)} %get-tuple-element.10.A_c, f32[2,128,128]{2,1,0:T(8,128)S(1)} %get-tuple-element.11.C_c, f32[2,2,128]{2,1,0:T(2,128)S(1)} %get-tuple-element.12.flux_ref), custom_call_target="tpu_custom_call" | custom-call | tf_op jit(solution)/shard_map/pallas_call | solution.py:491
